TPU v7x, 128 devices: a whole 4x4x4 slice. The times are simulated.
128 devices in a mesh: tx: 32 (over y, x, core), ty: 4 (over z).
Axes of the slice: x: 4, y: 4, z: 4, core: 2. Of those that a mesh axis runs over, the one named last changes fastest.
Arguments:
- points: bfloat16 [524288, 128], P(('tx', 'ty')), may hold values from -6 to 6
- embed_weight: bfloat16 [128, 512], replicated, may hold values from -0.5 to 0.5
- inner_weights: bfloat16 [1, 512, 512], replicated, may hold values from -0.25 to 0.25
- output_weight: bfloat16 [512, 128], replicated, may hold values from -0.25 to 0.25
- counts: int32 [128, 512], replicated, may hold values from 1 to 16, as said below
- point_order: int32 [128, 4096], P(('tx', 'ty')), may hold values from 0 to 4095, each once within a row
- inducing: bfloat16 [128, 128], replicated, may hold values from -6 to 6
- first_proj: bfloat16 [4, 128, 128], replicated, may hold values from -0.5 to 0.5
- second_proj: bfloat16 [4, 128, 128], replicated, may hold values from -0.5 to 0.5
- mixing: bfloat16 [8, 128, 128], replicated, may hold values from -0.1875 to 0.1875
Outputs:
- encoded: bfloat16 [524288, 128], P(('tx', 'ty'))
Inputs may be any that keep to these rules, and one draw needn't show every extreme that they name: Row s sums to 4096. For every source s and every device, the counts of s in the 4 tiles that device holds sum to exactly 32, and one of those 4 entries equals 16. Row s is a permutation of the local points of source s: the points of tile g are point_order[s, offsets[s, g] + c] for c below counts[s, g].
All inputs are finite; a program needn't handle non-finite values.
Results may differ from a plain program's by a relative error of at most 0.025.
Values may be sent and summed in bfloat16 or wider, within the bound.
A program may use at most 64 MiB of HBM per device.

v0:
```python
import math
import jax
import jax.numpy as jnp
from jax import lax
from jax.sharding import PartitionSpec as P

HEADS = 2
TLX = 2
TLY = 2
sharpness = 32.0
epsilon = 1e-06
neighbour_steps = ((-1, -1), (-1, 0), (-1, 1), (0, -1), (0, 1), (1, -1), (1, 0), (1, 1))


def padded_2(block, sides, width):
    for axis, dim in sides:
        count = lax.axis_size(axis)
        forward = [(i, i + 1) for i in range(count - 1)]
        backward = [(target, source) for source, target in forward]
        low = lax.ppermute(
            lax.slice_in_dim(block, block.shape[dim] - width, None, axis=dim), axis, forward
        )
        high = lax.ppermute(lax.slice_in_dim(block, 0, width, axis=dim), axis, backward)
        block = jnp.concatenate([low, block, high], axis=dim)
    return block


def unit_heads(projected, head_count):
    pieces = projected.reshape(
        projected.shape[:-1] + (head_count, projected.shape[-1] // head_count)
    )
    magnitude = jnp.sqrt(jnp.sum(pieces * pieces, axis=-1, keepdims=True) + epsilon)
    return (pieces / magnitude).reshape(projected.shape).astype(jnp.bfloat16)


def attend(query_rows, key_rows, value_rows, weight_mask):
    head_width = query_rows.shape[-1] // HEADS
    outputs = []
    for head_id in range(HEADS):
        lower = head_id * head_width
        upper = lower + head_width
        scores = jnp.dot(
            query_rows[:, lower:upper],
            key_rows[:, lower:upper].T,
            preferred_element_type=jnp.float32,
        )
        weights = jnp.exp(sharpness * scores) * weight_mask[None, :]
        totals = jnp.sum(weights, axis=1, keepdims=True)
        numer = jnp.dot(
            weights.astype(jnp.bfloat16),
            value_rows[:, lower:upper],
            preferred_element_type=jnp.float32,
        )
        outputs.append(numer / totals)
    return jnp.concatenate(outputs, axis=1).astype(jnp.bfloat16)


def block_layout(tallies, quota):
    before = jnp.cumsum(tallies, axis=0) - tallies
    through = (before + tallies).T
    slot_ids = jnp.arange(quota, dtype=jnp.int32)
    which = jnp.sum((slot_ids[None, :, None] >= through[:, None, :]).astype(jnp.int32), axis=2)
    base = jnp.take_along_axis(before.T, which, axis=1)
    return (before, which, slot_ids[None, :] - base)


def local_rows(index, source_rows, block):
    column_ids = jnp.arange(source_rows.shape[0], dtype=jnp.int32)

    def pick_block(index_block):
        table = (index_block[:, None] == column_ids[None, :]).astype(jnp.bfloat16)
        return jnp.dot(table, source_rows, preferred_element_type=jnp.float32).astype(jnp.bfloat16)

    picked = lax.map(pick_block, index.reshape(-1, block))
    return picked.reshape(index.shape[0], source_rows.shape[1])


def place_rows(index, rows, total, block):
    target_ids = jnp.arange(total, dtype=jnp.int32).reshape(-1, block)

    def place_block(target_block):
        table = (target_block[:, None] == index[None, :]).astype(jnp.bfloat16)
        return jnp.dot(table, rows, preferred_element_type=jnp.float32).astype(jnp.bfloat16)

    placed = lax.map(place_block, target_ids)
    return placed.reshape(total, rows.shape[1])


def slot_table(tallies, before, capacity, quota):
    slot_ids = jnp.arange(capacity, dtype=jnp.int32)
    packed_ids = jnp.arange(quota, dtype=jnp.int32)
    starts = before.T
    live = slot_ids[None, None, :] < tallies.T[:, :, None]
    hits = (
        packed_ids[None, None, None, :] == starts[:, :, None, None] + slot_ids[None, None, :, None]
    )
    return (hits & live[..., None]).astype(jnp.bfloat16)


def expand(blocks, table):
    return jnp.einsum("otcq,oqe->toce", table, blocks, preferred_element_type=jnp.float32).astype(
        jnp.bfloat16
    )


def collapse(slots, table):
    return jnp.einsum("otcq,toce->oqe", table, slots, preferred_element_type=jnp.float32).astype(
        jnp.bfloat16
    )


def body(
    points,
    embed_weight,
    inner_weights,
    output_weight,
    counts,
    point_order,
    inducing,
    first_proj,
    second_proj,
    mixing,
):
    along_x = lax.axis_size("tx")
    along_y = lax.axis_size("ty")
    devices = along_x * along_y
    index_x = lax.axis_index("tx")
    index_y = lax.axis_index("ty")
    own_index = index_x * along_y + index_y
    point_count = points.shape[0]
    capacity = 2 * point_count // counts.shape[1]
    per_device = TLX * TLY
    width = output_weight.shape[1]
    tile_rows = devices * capacity
    quota = point_count // devices
    block = math.gcd(512, point_count)
    hidden = jax.nn.silu(jnp.dot(points, embed_weight, preferred_element_type=jnp.float32)).astype(
        jnp.bfloat16
    )
    hidden = jax.nn.silu(
        jnp.dot(hidden, inner_weights[0], preferred_element_type=jnp.float32)
    ).astype(jnp.bfloat16)
    features = jnp.dot(hidden, output_weight, preferred_element_type=jnp.float32).astype(
        jnp.bfloat16
    )
    own_counts = lax.dynamic_index_in_dim(counts, own_index, 0, keepdims=False)
    own_offsets = jnp.cumsum(own_counts) - own_counts

    def by_owner(table):
        return (
            table.reshape(along_x, TLX, along_y, TLY)
            .transpose(1, 3, 0, 2)
            .reshape(per_device, devices)
        )

    slot_ids = jnp.arange(capacity, dtype=jnp.int32)
    send_counts = by_owner(own_counts)
    send_starts = by_owner(own_offsets)
    inbound = counts.reshape(devices, along_x, TLX, along_y, TLY)
    inbound = lax.dynamic_index_in_dim(inbound, index_x, 1, keepdims=False)
    inbound = lax.dynamic_index_in_dim(inbound, index_y, 2, keepdims=False)
    inbound = inbound.transpose(1, 2, 0).reshape(per_device, devices)
    live_slots = slot_ids[None, None, :] < inbound[:, :, None]
    key_mask = live_slots.astype(jnp.float32).reshape(per_device, tile_rows)
    send_before, send_which, send_within = block_layout(send_counts, quota)
    packed_pos = jnp.take_along_axis(send_starts.T, send_which, axis=1) + send_within
    packed_index = point_order[0][packed_pos].reshape(-1)
    packed = local_rows(packed_index, features, block).reshape(devices, quota, width)
    send_table = slot_table(send_counts, send_before, capacity, quota)
    outgoing = expand(packed, send_table)
    arrived = lax.all_to_all(outgoing, ("tx", "ty"), split_axis=1, concat_axis=1, tiled=True)
    arrived = arrived.reshape(per_device, tile_rows, width)
    all_rows = arrived.reshape(per_device * tile_rows, width)
    first_keys = unit_heads(
        jnp.dot(all_rows, first_proj[1], preferred_element_type=jnp.float32), HEADS
    ).reshape(per_device, tile_rows, width)
    first_values = (
        jnp.dot(all_rows, first_proj[2], preferred_element_type=jnp.float32)
        .astype(jnp.bfloat16)
        .reshape(per_device, tile_rows, width)
    )
    inducing_queries = unit_heads(
        jnp.dot(inducing, first_proj[0], preferred_element_type=jnp.float32), HEADS
    )
    first_attended = jax.vmap(attend, in_axes=(None, 0, 0, 0))(
        inducing_queries, first_keys, first_values, key_mask
    )
    summary = (
        inducing.astype(jnp.float32)[None]
        + jnp.einsum(
            "tic,ce->tie", first_attended, first_proj[3], preferred_element_type=jnp.float32
        )
    ).astype(jnp.bfloat16)
    tile_grid = summary.reshape(TLX, TLY, summary.shape[1], width)
    padded = padded_2(tile_grid, (("tx", 0), ("ty", 1)), 1)
    stacked = jnp.stack(
        [
            padded[1 + steps[0] : 1 + steps[0] + TLX, 1 + steps[1] : 1 + steps[1] + TLY]
            for steps in neighbour_steps
        ]
    )
    mixture = tile_grid.astype(jnp.float32) + jnp.einsum(
        "dxyic,dce->xyie", stacked, mixing, preferred_element_type=jnp.float32
    )
    mixture = mixture.astype(jnp.bfloat16).reshape(per_device * summary.shape[1], width)
    point_queries = unit_heads(
        jnp.dot(all_rows, second_proj[0], preferred_element_type=jnp.float32), HEADS
    ).reshape(per_device, tile_rows, width)
    second_keys = unit_heads(
        jnp.dot(mixture, second_proj[1], preferred_element_type=jnp.float32), HEADS
    ).reshape(per_device, -1, width)
    second_values = (
        jnp.dot(mixture, second_proj[2], preferred_element_type=jnp.float32)
        .astype(jnp.bfloat16)
        .reshape(per_device, -1, width)
    )
    every_key = jnp.ones((second_keys.shape[1],), jnp.float32)
    second_attended = jax.vmap(attend, in_axes=(0, 0, 0, None))(
        point_queries, second_keys, second_values, every_key
    )
    result = (
        arrived.astype(jnp.float32)
        + jnp.einsum(
            "trc,ce->tre", second_attended, second_proj[3], preferred_element_type=jnp.float32
        )
    ).astype(jnp.bfloat16)
    result_slots = result.reshape(per_device, devices, capacity, width)
    coming = lax.all_to_all(result_slots, ("tx", "ty"), split_axis=1, concat_axis=1, tiled=True)
    returned = collapse(coming, send_table)
    return place_rows(packed_index, returned.reshape(point_count, width), point_count, block)


def solution(mesh):
    placed = (P(("tx", "ty"), None), P(), P(), P(), P(), P(("tx", "ty"), None), P(), P(), P(), P())
    return jax.shard_map(
        body, mesh=mesh, in_specs=placed, out_specs=P(("tx", "ty"), None), check_vma=False
    )
```

profile of v0, /device:TPU:1, one launch (start us, length us, event | category | flops | bytes accessed | tf_op | source)
XLA Modules:
  0.0 279.4 jit_solution(15943603343116851955)
XLA Ops:
  0.0 0.5 broadcast.183
  0.5 1.4 fusion.117
  3.1 0.5 copy.58
  3.8 0.5 copy.55
  5.2 26.7 %gather_fusion.2 = s32[4096]{0:T(1024)S(1)} fusion(s32[128,4]{1,0:T(8,128)S(1)} %subtract_bitcast_fusion.1, s32[4096]{0:T(1024)S(1)} %reshape.218), kind=kCustom, calls=%fused_computation.1.clone | custom fusion | bytes 65536 | tf_op jit(solution)/shard_map/jit(take_along_axis)/gather | solution.py:63
  31.9 33.1 %gather_fusion.1 = s32[4096]{0:T(1024)S(1)} fusion(s32[128,4]{0,1:T(4,128)S(1)} %bitcast.236, s32[4096]{0:T(1024)S(1)} %reshape.218), kind=kCustom, calls=%fused_computation.clone | custom fusion | bytes 65536 | tf_op jit(solution)/shard_map/jit(take_along_axis)/gather | solution.py:166
  65.8 23.0 %gather_fusion = s32[4096]{0:T(1024)S(1)} fusion(s32[4096]{0:T(1024)S(1)} %bitcast.237, s32[4096]{0:T(1024)S(1)} %broadcast_clamp_fusion), kind=kCustom, calls=%fused_computation.2 | custom fusion | bytes 49152 | tf_op jit(solution)/shard_map/gather | solution.py:167
  88.9 6.4 %fusion.21 = f32[4096,512]{1,0:T(8,128)} fusion(bf16[4096,128]{1,0:T(8,128)(2,1)S(1)} %copy-done, bf16[128,512]{1,0:T(8,128)(2,1)S(1)} %copy-done.18, bf16[1,512,512]{2,1,0:T(8,128)(2,1)S(1)} %copy-done.17), kind=kOutput, calls=%fused_computation.38 | convolution fusion | flops 2694840320 | bytes 10092544 | tf_op jit(solution)/shard_map/dot_general | solution.py:141
  95.3 5.7 %convolution_convert_fusion.1 = bf16[4096,128]{1,0:T(8,128)(2,1)S(1)} fusion(bf16[512,128]{1,0:T(8,128)(2,1)S(1)} %copy-done.19, f32[4096,512]{1,0:T(8,128)} %fusion.21), kind=kOutput, calls=%fused_computation.22 | convolution fusion | flops 547880960 | bytes 9568256 | tf_op jit(solution)/shard_map/dot_general | solution.py:143
  101.1 12.9 %while.22 = (s32[]{:T(128)}, bf16[8,512,128]{2,1,0:T(8,128)(2,1)S(1)}, s32[8,512]{1,0:T(8,128)S(1)}, bf16[4096,128]{1,0:T(8,128)(2,1)S(1)}, s32[]{:T(128)}) while((s32[]{:T(128)}, bf16[8,512,128]{2,1,0:T(8,128)(2,1)S(1)}, s32[8,512]{1,0:T(8,128)S(1)}, bf16[4096,128]{1,0:T(8,128)(2,1)S(1)}, s32[]{:T(128)}) %tuple.56), condition=%wide.region_5.7_spmd.clone, body=%wide.region_4.6_spmd.clone.sunk | while | flops 539033600 | bytes 1185861 | solution.py:74
  101.1 1.6 fusion.148
  102.8 1.6 fusion.148
  104.4 1.6 fusion.148
  106.0 1.6 fusion.148
  107.6 1.6 fusion.148
  109.2 1.6 fusion.148
  110.8 1.6 fusion.148
  112.4 1.6 fusion.148
  114.4 5.1 %convert_bitcast_fusion = bf16[4,128,16,128]{3,2,0,1:T(8,128)(2,1)} fusion(bf16[128,32,128,1]{2,1,3,0:T(8,128)(2,1)S(1)} %bitcast.252, s32[128,4,16]{2,1,0:T(4,128)S(1)} %iota_add_fusion, pred[128,4,16]{2,1,0:T(4,128)(4,1)S(1)} %iota_compare_fusion.9), kind=kOutput, calls=%fused_computation.65 | convolution fusion | flops 68681728 | bytes 3186688 | tf_op jit(solution)/shard_map/otcq,oqe->toce/dot_general | solution.py:101
  119.5 12.0 %all-to-all-start = ((bf16[4,128,16,128]{3,2,0,1:T(8,128)(2,1)}), bf16[4,128,16,128]{3,2,0,1:T(8,128)(2,1)}, u32[]{:S(2)}, u32[]{:S(2)}) async-start(bf16[4,128,16,128]{3,2,0,1:T(8,128)(2,1)} %convert_bitcast_fusion), calls=%async_computation | async-start | bytes 4194304 | tf_op jit(solution)/shard_map/all_to_all | solution.py:171
  132.4 0.7 copy.85
  133.4 0.6 compare_convert_fusion
  134.1 27.6 %all-to-all-done = bf16[4,128,16,128]{3,2,0,1:T(8,128)(2,1)} async-done(((bf16[4,128,16,128]{3,2,0,1:T(8,128)(2,1)}), bf16[4,128,16,128]{3,2,0,1:T(8,128)(2,1)}, u32[]{:S(2)}, u32[]{:S(2)}) %all-to-all-start) | async-done | bytes 2097184 | tf_op jit(solution)/shard_map/all_to_all | solution.py:171
  161.7 2.0 copy.67
  163.6 0.7 multiply_reduce_fusion
  164.5 1.7 divide_convert_fusion
  166.1 4.5 %convert_element_type.119 = bf16[4,2048,128]{1,0,2:T(4,128)(2,1)} reshape(bf16[8192,2,64]{0,2,1:T(8,128)(2,1)} %divide_convert_fusion) | data formatting | bytes 4194304 | tf_op jit(solution)/shard_map/convert_element_type | solution.py:33
  170.6 2.5 fusion.119
  173.2 0.7 convolution_convert_fusion
  173.9 1.6 fusion.77
  175.5 2.7 bitcast_reduce_fusion.1
  178.2 1.9 fusion.64
  180.1 1.1 fusion.70
  181.5 2.8 collective-permute-start
  184.3 2.1 collective-permute-start.1
  186.4 0.7 multiply_reduce_fusion.1
  187.3 0.4 divide_convert_fusion.1
  187.6 2.8 convert_element_type.114
  190.5 2.5 collective-permute-start.2
  192.9 1.3 collective-permute-start.3
  194.2 2.6 fusion.118
  196.8 3.9 %copy.66 = f32[4,128,16,128]{3,2,1,0:T(8,128)} copy(bf16[4,128,16,128]{3,2,0,1:T(8,128)(2,1)} %all-to-all-done) | data formatting | bytes 6291456 | tf_op jit(solution)/shard_map/convert_element_type | solution.py:222
  201.1 0.4 fusion.60
  202.1 2.0 fusion.27
  204.1 2.0 fusion.29
  206.1 0.9 fusion.33
  207.1 0.9 fusion.34
  208.0 1.3 copy-done.3
  209.2 0.8 fusion.20
  210.1 2.0 copy.94
  212.1 8.4 %all-to-all-start.1 = ((bf16[4,128,16,128]{3,2,0,1:T(8,128)(2,1)}), bf16[4,128,16,128]{3,2,0,1:T(8,128)(2,1)S(1)}, u32[]{:S(2)}, u32[]{:S(2)}) async-start(bf16[4,128,16,128]{3,2,0,1:T(8,128)(2,1)} %copy.94), calls=%async_computation.1 | async-start | bytes 4194304 | tf_op jit(solution)/shard_map/all_to_all | solution.py:228
  220.7 30.4 %all-to-all-done.1 = bf16[4,128,16,128]{3,2,0,1:T(8,128)(2,1)S(1)} async-done(((bf16[4,128,16,128]{3,2,0,1:T(8,128)(2,1)}), bf16[4,128,16,128]{3,2,0,1:T(8,128)(2,1)S(1)}, u32[]{:S(2)}, u32[]{:S(2)}) %all-to-all-start.1) | async-done | bytes 2097184 | tf_op jit(solution)/shard_map/all_to_all | solution.py:228
  251.0 5.7 %bitcast_convert_fusion.4 = bf16[128,32,128]{2,1,0:T(8,128)(2,1)} fusion(bf16[4,128,16,128]{3,2,0,1:T(8,128)(2,1)S(1)} %all-to-all-done.1, s32[128,4,16]{2,1,0:T(4,128)S(1)} %iota_add_fusion, pred[128,4,16]{2,1,0:T(4,128)(4,1)S(1)} %copy-done.16), kind=kOutput, calls=%fused_computation.58 | convolution fusion | flops 68157440 | bytes 3186688 | tf_op jit(solution)/shard_map/otcq,toce->oqe/dot_general | solution.py:107
  256.8 20.9 %while.23 = (s32[]{:T(128)}, bf16[8,512,128]{2,1,0:T(8,128)(2,1)S(1)}, s32[8,512]{1,0:T(8,128)S(1)}, s32[128,32]{1,0:T(8,128)}, bf16[4096,128]{1,0:T(8,128)(2,1)}, /*index=5*/s32[4096]{0:T(1024)S(1)}, s32[]{:T(128)}) while((s32[]{:T(128)}, bf16[8,512,128]{2,1,0:T(8,128)(2,1)S(1)}, s32[8,512]{1,0:T(8,128)S(1)}, ...), condition=%wide.wide.region_15.17_spmd, body=%wide.wide.region_14.16_spmd.sunk | while | flops 539033600 | bytes 1202261 | solution.py:85
  256.9 2.6 fusion.151
  259.5 2.6 fusion.151
  262.1 2.6 fusion.151
  264.7 2.6 fusion.151
  267.3 2.6 fusion.151
  269.9 2.6 fusion.151
  272.6 2.6 fusion.151
  275.2 2.6 fusion.151
  277.8 0.9 copy-done.4
  278.7 0.6 copy-done.1
  (129 shorter events, 6.1 us)
Async XLA Ops:
  0.0 88.8 %copy-start = (bf16[4096,128]{1,0:T(8,128)(2,1)S(1)}, bf16[4096,128]{1,0:T(8,128)(2,1)}, u32[]{:S(2)}) copy-start(bf16[4096,128]{1,0:T(8,128)(2,1)} %param.16) | copy-start | bytes 3145732
  65.1 0.7 copy-start.2
  65.8 23.1 %copy-start.17 = (bf16[1,512,512]{2,1,0:T(8,128)(2,1)S(1)}, bf16[1,512,512]{2,1,0:T(8,128)(2,1)}, u32[]{:S(2)}) copy-start(bf16[1,512,512]{2,1,0:T(8,128)(2,1)} %param.18) | copy-start | bytes 1572868
  65.8 23.1 %copy-start.18 = (bf16[128,512]{1,0:T(8,128)(2,1)S(1)}, bf16[128,512]{1,0:T(8,128)(2,1)}, u32[]{:S(2)}) copy-start(bf16[128,512]{1,0:T(8,128)(2,1)} %param.17) | copy-start | bytes 393220
  88.9 6.4 %copy-start.19 = (bf16[512,128]{1,0:T(8,128)(2,1)S(1)}, bf16[512,128]{1,0:T(8,128)(2,1)}, u32[]{:S(2)}) copy-start(bf16[512,128]{1,0:T(8,128)(2,1)} %param.19) | copy-start | bytes 393220
  114.3 5.1 %copy-start.15 = (pred[128,4,16]{2,1,0:T(4,128)(4,1)}, pred[128,4,16]{2,1,0:T(4,128)(4,1)S(1)}, u32[]{:S(2)}) copy-start(pred[128,4,16]{2,1,0:T(4,128)(4,1)S(1)} %iota_compare_fusion.9) | copy-start | bytes 24580
  119.5 12.0 %copy-start.5 = (s32[128,512]{1,0:T(8,128)S(1)}, s32[128,512]{1,0:T(8,128)}, u32[]{:S(2)}) copy-start(s32[128,512]{1,0:T(8,128)} %param.20) | copy-start | bytes 786436
  119.5 12.2 %copy-start.11 = (bf16[4,128,128]{2,1,0:T(8,128)(2,1)S(1)}, bf16[4,128,128]{2,1,0:T(8,128)(2,1)}, u32[]{:S(2)}) copy-start(bf16[4,128,128]{2,1,0:T(8,128)(2,1)} %param.23) | copy-start | bytes 393220
  119.5 12.8 %copy-start.13 = (bf16[128,128]{1,0:T(8,128)(2,1)S(1)}, bf16[128,128]{1,0:T(8,128)(2,1)}, u32[]{:S(2)}) copy-start(bf16[128,128]{1,0:T(8,128)(2,1)} %param.22) | copy-start | bytes 98308
  119.5 12.8 %copy-start.9 = (bf16[4,128,128]{2,1,0:T(8,128)(2,1)S(1)}, bf16[4,128,128]{2,1,0:T(8,128)(2,1)}, u32[]{:S(2)}) copy-start(bf16[4,128,128]{2,1,0:T(8,128)(2,1)} %param.24) | copy-start | bytes 393220
  119.5 42.2 %all-to-all-start = ((bf16[4,128,16,128]{3,2,0,1:T(8,128)(2,1)}), bf16[4,128,16,128]{3,2,0,1:T(8,128)(2,1)}, u32[]{:S(2)}, u32[]{:S(2)}) async-start(bf16[4,128,16,128]{3,2,0,1:T(8,128)(2,1)} %convert_bitcast_fusion), calls=%async_computation | async-start | bytes 4194304 | tf_op jit(solution)/shard_map/all_to_all | solution.py:171
  170.6 2.5 copy-start.12
  173.8 1.7 copy-start.8
  181.5 8.9 %collective-permute-start = (bf16[1,2,128,128]{3,2,1,0:T(8,128)(2,1)S(1)}, bf16[1,2,128,128]{3,2,1,0:T(8,128)(2,1)S(1)}, u32[]{:S(2)}, u32[]{:S(2)}) collective-permute-start(bf16[1,2,128,128]{3,2,1,0:T(8,128)(2,1)S(1)} %get-tuple-element.106), channel_id=1, source_target_pairs={{0,4},{4,8},{8,12},{12,16},{16,20},{20,24},{24,28},{28,32},{32,36}... | collective-permute-start | bytes 196616 | tf_op jit(solution)/shard_map/ppermute | solution.py:20
  184.3 6.1 %collective-permute-start.1 = (bf16[1,2,128,128]{3,2,1,0:T(8,128)(2,1)S(1)}, bf16[1,2,128,128]{3,2,1,0:T(8,128)(2,1)S(1)}, u32[]{:S(2)}, u32[]{:S(2)}) collective-permute-start(bf16[1,2,128,128]{3,2,1,0:T(8,128)(2,1)S(1)} %get-tuple-element.107), channel_id=1, source_target_pairs={{4,0},{8,4},{12,8},{16,12},{20,16},{24,20},{28,24},{32,28},{36,32}... | collective-permute-start | bytes 196616 | tf_op jit(solution)/shard_map/ppermute | solution.py:23
  190.5 10.3 %collective-permute-start.2 = (bf16[4,1,128,128]{3,2,1,0:T(8,128)(2,1)S(1)}, bf16[4,1,128,128]{3,2,1,0:T(8,128)(2,1)S(1)}, u32[]{:S(2)}, u32[]{:S(2)}) collective-permute-start(bf16[4,1,128,128]{3,2,1,0:T(8,128)(2,1)S(1)} %get-tuple-element.101), channel_id=1, source_target_pairs={{0,1},{1,2},{2,3},{4,5},{5,6},{6,7},{8,9},{9,10},{10,11},{12,13},{... | collective-permute-start | bytes 393224 | tf_op jit(solution)/shard_map/ppermute | solution.py:20
  192.9 7.8 %collective-permute-start.3 = (bf16[4,1,128,128]{3,2,1,0:T(8,128)(2,1)S(1)}, bf16[4,1,128,128]{3,2,1,0:T(8,128)(2,1)S(1)}, u32[]{:S(2)}, u32[]{:S(2)}) collective-permute-start(bf16[4,1,128,128]{3,2,1,0:T(8,128)(2,1)S(1)} %get-tuple-element.100), channel_id=1, source_target_pairs={{1,0},{2,1},{3,2},{5,4},{6,5},{7,6},{9,8},{10,9},{11,10},{13,12},{... | collective-permute-start | bytes 393224 | tf_op jit(solution)/shard_map/ppermute | solution.py:23
  196.8 4.2 %copy-start.7 = (bf16[8,128,128]{2,1,0:T(8,128)(2,1)S(1)}, bf16[8,128,128]{2,1,0:T(8,128)(2,1)}, u32[]{:S(2)}) copy-start(bf16[8,128,128]{2,1,0:T(8,128)(2,1)} %param.25) | copy-start | bytes 786436
  196.8 4.7 %copy-start.14 = (bf16[128,128]{1,0:T(8,128)(2,1)S(1)}, bf16[128,128]{1,0:T(8,128)(2,1)}, u32[]{:S(2)}) copy-start(bf16[128,128]{1,0:T(8,128)(2,1)} %copy.85) | copy-start | bytes 98308
  200.8 1.1 copy-start.10
  207.1 2.2 copy-start.3
  210.1 41.0 %copy-start.16 = (pred[128,4,16]{2,1,0:T(4,128)(4,1)S(1)}, pred[128,4,16]{2,1,0:T(4,128)(4,1)}, u32[]{:S(2)}) copy-start(pred[128,4,16]{2,1,0:T(4,128)(4,1)} %copy-done.15) | copy-start | bytes 24580
  212.1 39.0 %all-to-all-start.1 = ((bf16[4,128,16,128]{3,2,0,1:T(8,128)(2,1)}), bf16[4,128,16,128]{3,2,0,1:T(8,128)(2,1)S(1)}, u32[]{:S(2)}, u32[]{:S(2)}) async-start(bf16[4,128,16,128]{3,2,0,1:T(8,128)(2,1)} %copy.94), calls=%async_computation.1 | async-start | bytes 4194304 | tf_op jit(solution)/shard_map/all_to_all | solution.py:228
  220.6 36.1 %copy-start.6 = (s32[128,32]{1,0:T(8,128)}, s32[128,32]{1,0:T(8,128)S(1)}, u32[]{:S(2)}) copy-start(s32[128,32]{1,0:T(8,128)S(1)} %reshape.197) | copy-start | bytes 49156
  277.8 1.0 copy-start.4
  277.8 1.6 copy-start.1
where the time goes:
time: 280 us; the launch traced here: 279 us
  local copies, waits for them, and re-layouts  113 us (40%)
  matrix products  73.6 us (26%)
  waiting for transfers between devices  58 us (21%)
  starting transfers between devices  29.1 us (10%)
  other arithmetic  4.16 us (1%)
    gather x5, local copies, waits for them, and re-layouts, body(): jnp.take_along_axis(send_starts.T, send_which, axis=1) + send_within  33.4 us
    all_to_all x1, waiting for transfers between devices, body(): lax.all_to_all(result_slots, ('tx', 'ty'), split_axis=1, concat_axis=1, t...  30.4 us
    all_to_all x1, waiting for transfers between devices, body(): lax.all_to_all(outgoing, ('tx', 'ty'), split_axis=1, concat_axis=1, tiled...  27.6 us
    gather x3, local copies, waits for them, and re-layouts, block_layout(): base = jnp.take_along_axis(before.T, which, axis=1)  26.9 us
    gather x2, local copies, waits for them, and re-layouts, body(): packed_index = point_order[0][packed_pos].reshape(-1)  23.1 us
    dot_general x8, matrix products, place_block(): jnp.dot(table, rows, preferred_element_type=jnp.float32)  20.7 us
    dot_general x8, matrix products, pick_block(): jnp.dot(table, source_rows, preferred_element_type=jnp.float32)  12.7 us
    all_to_all x1, starting transfers between devices, body(): lax.all_to_all(outgoing, ('tx', 'ty'), split_axis=1, concat_axis=1, tiled...  12 us
  transfers between devices with their start and end apart: 6, of which 2 were waited for; matrix products, arithmetic and copies ran while one was open for 5% of the time, Pallas kernels for 0%

commit v1 on v0

--- a/solution.py
+++ b/solution.py
@@ -225,7 +225,15 @@
         )
     ).astype(jnp.bfloat16)
     result_slots = result.reshape(per_device, devices, capacity, width)
-    coming = lax.all_to_all(result_slots, ("tx", "ty"), split_axis=1, concat_axis=1, tiled=True)
+    coming = jnp.concatenate(
+        lax.all_to_all(
+            jnp.stack(jnp.split(result_slots, lax.axis_size(("tx", "ty")), axis=1)),
+            ("tx", "ty"),
+            0,
+            0,
+        ),
+        axis=1,
+    )
     returned = collapse(coming, send_table)
     return place_rows(packed_index, returned.reshape(point_count, width), point_count, block)
 

time: 280 us -> 356 us (1.27)
  local copies, waits for them, and re-layouts: 113 us -> 189 us
    unnamed x46 -> x173, local copies, waits for them, and re-layouts: 3.35 us -> 80.3 us
  transfers between devices with their start and end apart: 6 -> 6, of which waited for: 2 -> 2; matrix products, arithmetic and copies ran while one was open for 5% -> 4% of each run, Pallas kernels for 0% -> 0%
where the time goes in v1:
time: 356 us; the launch traced here: 355 us
  local copies, waits for them, and re-layouts  189 us (53%)
  matrix products  73.6 us (21%)
  waiting for transfers between devices  58 us (16%)
  starting transfers between devices  29.1 us (8%)
  other arithmetic  4.16 us (1%)
    unnamed x173, local copies, waits for them, and re-layouts  80.3 us
    gather x5, local copies, waits for them, and re-layouts, body(): jnp.take_along_axis(send_starts.T, send_which, axis=1) + send_within  33.4 us
    all_to_all x1, waiting for transfers between devices, body(): lax.all_to_all(jnp.stack(jnp.split(result_slots, lax.axis_size(('tx', 'ty...  30.4 us
    all_to_all x1, waiting for transfers between devices, body(): lax.all_to_all(outgoing, ('tx', 'ty'), split_axis=1, concat_axis=1, tiled...  27.6 us
    gather x3, local copies, waits for them, and re-layouts, block_layout(): base = jnp.take_along_axis(before.T, which, axis=1)  26.9 us
    gather x2, local copies, waits for them, and re-layouts, body(): packed_index = point_order[0][packed_pos].reshape(-1)  23.1 us
    dot_general x8, matrix products, place_block(): jnp.dot(table, rows, preferred_element_type=jnp.float32)  20.7 us
    dot_general x8, matrix products, pick_block(): jnp.dot(table, source_rows, preferred_element_type=jnp.float32)  12.7 us
  transfers between devices with their start and end apart: 6, of which 2 were waited for; matrix products, arithmetic and copies ran while one was open for 4% of the time, Pallas kernels for 0%

profile of v1, /device:TPU:1, one launch (start us, length us, event | category | flops | bytes accessed | tf_op | source)
XLA Modules:
  0.0 355.0 jit_solution(17868853047802596054)
XLA Ops:
  0.5 1.4 fusion.112
  5.2 26.7 %gather_fusion.2 = s32[4096]{0:T(1024)S(1)} fusion(s32[128,4]{1,0:T(8,128)S(1)} %subtract_bitcast_fusion.1, s32[4096]{0:T(1024)S(1)} %reshape.226), kind=kCustom, calls=%fused_computation.1.clone | custom fusion | bytes 65536 | tf_op jit(solution)/shard_map/jit(take_along_axis)/gather | solution.py:63
  31.9 33.1 %gather_fusion.1 = s32[4096]{0:T(1024)S(1)} fusion(s32[128,4]{0,1:T(4,128)S(1)} %bitcast.1012, s32[4096]{0:T(1024)S(1)} %reshape.226), kind=kCustom, calls=%fused_computation.clone | custom fusion | bytes 65536 | tf_op jit(solution)/shard_map/jit(take_along_axis)/gather | solution.py:166
  65.8 23.0 %gather_fusion = s32[4096]{0:T(1024)S(1)} fusion(s32[4096]{0:T(1024)S(1)} %bitcast.1013, s32[4096]{0:T(1024)S(1)} %broadcast_clamp_fusion), kind=kCustom, calls=%fused_computation.2 | custom fusion | bytes 49152 | tf_op jit(solution)/shard_map/gather | solution.py:167
  88.9 6.4 %fusion.21 = f32[4096,512]{1,0:T(8,128)} fusion(bf16[4096,128]{1,0:T(8,128)(2,1)S(1)} %copy-done, bf16[128,512]{1,0:T(8,128)(2,1)S(1)} %copy-done.18, bf16[1,512,512]{2,1,0:T(8,128)(2,1)S(1)} %copy-done.17), kind=kOutput, calls=%fused_computation.38 | convolution fusion | flops 2694840320 | bytes 10092544 | tf_op jit(solution)/shard_map/dot_general | solution.py:141
  95.3 5.7 %convolution_convert_fusion.1 = bf16[4096,128]{1,0:T(8,128)(2,1)S(1)} fusion(bf16[512,128]{1,0:T(8,128)(2,1)S(1)} %copy-done.19, f32[4096,512]{1,0:T(8,128)} %fusion.21), kind=kOutput, calls=%fused_computation.22 | convolution fusion | flops 547880960 | bytes 9568256 | tf_op jit(solution)/shard_map/dot_general | solution.py:143
  101.1 12.9 %while.22 = (s32[]{:T(128)}, bf16[8,512,128]{2,1,0:T(8,128)(2,1)S(1)}, s32[8,512]{1,0:T(8,128)S(1)}, bf16[4096,128]{1,0:T(8,128)(2,1)S(1)}, s32[]{:T(128)}) while((s32[]{:T(128)}, bf16[8,512,128]{2,1,0:T(8,128)(2,1)S(1)}, s32[8,512]{1,0:T(8,128)S(1)}, bf16[4096,128]{1,0:T(8,128)(2,1)S(1)}, s32[]{:T(128)}) %tuple.56), condition=%wide.region_5.7_spmd.clone, body=%wide.region_4.6_spmd.clone.sunk | while | flops 539033600 | bytes 1185861 | solution.py:74
  101.1 1.6 fusion.142
  102.8 1.6 fusion.142
  104.4 1.6 fusion.142
  106.0 1.6 fusion.142
  107.6 1.6 fusion.142
  109.2 1.6 fusion.142
  110.8 1.6 fusion.142
  112.4 1.6 fusion.142
  114.4 5.1 %convert_bitcast_fusion = bf16[4,128,16,128]{3,2,0,1:T(8,128)(2,1)} fusion(bf16[128,32,128,1]{2,1,3,0:T(8,128)(2,1)S(1)} %bitcast.1155, s32[128,4,16]{2,1,0:T(4,128)S(1)} %iota_add_fusion, pred[128,4,16]{2,1,0:T(4,128)(4,1)S(1)} %iota_compare_fusion.9), kind=kOutput, calls=%fused_computation.66 | convolution fusion | flops 68681728 | bytes 3186688 | tf_op jit(solution)/shard_map/otcq,oqe->toce/dot_general | solution.py:101
  119.5 12.0 %all-to-all-start = ((bf16[4,128,16,128]{3,2,0,1:T(8,128)(2,1)}), bf16[4,128,16,128]{3,2,0,1:T(8,128)(2,1)}, u32[]{:S(2)}, u32[]{:S(2)}) async-start(bf16[4,128,16,128]{3,2,0,1:T(8,128)(2,1)} %convert_bitcast_fusion), calls=%async_computation | async-start | bytes 4194304 | tf_op jit(solution)/shard_map/all_to_all | solution.py:171
  132.4 0.7 copy.501
  133.4 0.6 compare_convert_fusion
  134.1 27.6 %all-to-all-done = bf16[4,128,16,128]{3,2,0,1:T(8,128)(2,1)} async-done(((bf16[4,128,16,128]{3,2,0,1:T(8,128)(2,1)}), bf16[4,128,16,128]{3,2,0,1:T(8,128)(2,1)}, u32[]{:S(2)}, u32[]{:S(2)}) %all-to-all-start) | async-done | bytes 2097184 | tf_op jit(solution)/shard_map/all_to_all | solution.py:171
  161.7 2.0 copy.483
  163.6 0.7 multiply_reduce_fusion
  164.5 1.7 divide_convert_fusion
  166.1 4.5 %convert_element_type.119 = bf16[4,2048,128]{1,0,2:T(4,128)(2,1)} reshape(bf16[8192,2,64]{0,2,1:T(8,128)(2,1)} %divide_convert_fusion) | data formatting | bytes 4194304 | tf_op jit(solution)/shard_map/convert_element_type | solution.py:33
  170.6 2.5 fusion.114
  173.2 0.7 convolution_convert_fusion
  173.9 1.6 fusion.80
  175.5 2.7 bitcast_reduce_fusion.1
  178.2 1.9 fusion.67
  180.1 1.1 fusion.73
  181.5 2.8 collective-permute-start
  184.3 2.1 collective-permute-start.1
  186.4 0.7 multiply_reduce_fusion.1
  187.6 2.8 convert_element_type.114
  190.5 2.5 collective-permute-start.2
  192.9 1.3 collective-permute-start.3
  194.2 2.6 fusion.113
  196.8 3.9 %copy.482 = f32[4,128,16,128]{3,2,1,0:T(8,128)} copy(bf16[4,128,16,128]{3,2,0,1:T(8,128)(2,1)} %all-to-all-done) | data formatting | bytes 6291456 | tf_op jit(solution)/shard_map/convert_element_type | solution.py:222
  201.0 0.6 copy-done.7
  202.6 2.0 fusion.27
  204.7 2.0 fusion.29
  206.7 0.9 fusion.33
  207.6 0.9 fusion.34
  208.5 1.3 copy-done.3
  209.8 0.8 fusion.20
  214.2 0.6 constant_dynamic-update-slice_fusion.129
  244.3 0.6 constant_dynamic-update-slice_fusion.79
  248.6 0.6 constant_dynamic-update-slice_fusion.72
  252.8 0.6 constant_dynamic-update-slice_fusion.65
  254.6 0.6 constant_dynamic-update-slice_fusion.62
  287.7 8.4 %all-to-all-start.1 = ((bf16[128,4,1,16,128]{4,3,1,2,0:T(8,128)(2,1)}), bf16[128,4,1,16,128]{4,3,1,2,0:T(8,128)(2,1)S(1)}, u32[]{:S(2)}, u32[]{:S(2)}) async-start(bf16[128,4,1,16,128]{4,3,1,2,0:T(8,128)(2,1)} %constant_dynamic-update-slice_fusion.8), calls=%async_computation.1 | async-start | bytes 4194304 | tf_op jit(solution)/shard_map/all_to_all | solution.py:229
  296.3 30.4 %all-to-all-done.1 = bf16[128,4,1,16,128]{4,3,1,2,0:T(8,128)(2,1)S(1)} async-done(((bf16[128,4,1,16,128]{4,3,1,2,0:T(8,128)(2,1)}), bf16[128,4,1,16,128]{4,3,1,2,0:T(8,128)(2,1)S(1)}, u32[]{:S(2)}, u32[]{:S(2)}) %all-to-all-start.1) | async-done | bytes 2097184 | tf_op jit(solution)/shard_map/all_to_all | solution.py:229
  326.7 5.7 %bitcast_convert_fusion.4 = bf16[128,32,128]{2,1,0:T(8,128)(2,1)} fusion(bf16[128,4,1,16,128]{4,3,1,2,0:T(8,128)(2,1)S(1)} %all-to-all-done.1, s32[128,4,16]{2,1,0:T(4,128)S(1)} %iota_add_fusion, pred[128,4,16]{2,1,0:T(4,128)(4,1)S(1)} %copy-done.16), kind=kOutput, calls=%fused_computation.59 | convolution fusion | flops 68157440 | bytes 3186688 | tf_op jit(solution)/shard_map/otcq,toce->oqe/dot_general | solution.py:107
  332.5 20.9 %while.23 = (s32[]{:T(128)}, bf16[8,512,128]{2,1,0:T(8,128)(2,1)S(1)}, s32[8,512]{1,0:T(8,128)S(1)}, s32[128,32]{1,0:T(8,128)}, bf16[4096,128]{1,0:T(8,128)(2,1)}, /*index=5*/s32[4096]{0:T(1024)S(1)}, s32[]{:T(128)}) while((s32[]{:T(128)}, bf16[8,512,128]{2,1,0:T(8,128)(2,1)S(1)}, s32[8,512]{1,0:T(8,128)S(1)}, ...), condition=%wide.wide.region_15.17_spmd, body=%wide.wide.region_14.16_spmd.sunk | while | flops 539033600 | bytes 1202261 | solution.py:85
  332.5 2.6 fusion.145
  335.1 2.6 fusion.145
  337.7 2.6 fusion.145
  340.3 2.6 fusion.145
  342.9 2.6 fusion.145
  345.6 2.6 fusion.145
  348.2 2.6 fusion.145
  350.8 2.6 fusion.145
  353.4 0.9 copy-done.4
  354.4 0.6 copy-done.1
  (256 shorter events, 82.3 us)
Async XLA Ops:
  0.0 88.8 %copy-start = (bf16[4096,128]{1,0:T(8,128)(2,1)S(1)}, bf16[4096,128]{1,0:T(8,128)(2,1)}, u32[]{:S(2)}) copy-start(bf16[4096,128]{1,0:T(8,128)(2,1)} %param.16) | copy-start | bytes 3145732
  65.1 0.7 copy-start.2
  65.8 23.1 %copy-start.17 = (bf16[1,512,512]{2,1,0:T(8,128)(2,1)S(1)}, bf16[1,512,512]{2,1,0:T(8,128)(2,1)}, u32[]{:S(2)}) copy-start(bf16[1,512,512]{2,1,0:T(8,128)(2,1)} %param.18) | copy-start | bytes 1572868
  65.8 23.1 %copy-start.18 = (bf16[128,512]{1,0:T(8,128)(2,1)S(1)}, bf16[128,512]{1,0:T(8,128)(2,1)}, u32[]{:S(2)}) copy-start(bf16[128,512]{1,0:T(8,128)(2,1)} %param.17) | copy-start | bytes 393220
  88.9 6.4 %copy-start.19 = (bf16[512,128]{1,0:T(8,128)(2,1)S(1)}, bf16[512,128]{1,0:T(8,128)(2,1)}, u32[]{:S(2)}) copy-start(bf16[512,128]{1,0:T(8,128)(2,1)} %param.19) | copy-start | bytes 393220
  114.3 5.1 %copy-start.15 = (pred[128,4,16]{2,1,0:T(4,128)(4,1)}, pred[128,4,16]{2,1,0:T(4,128)(4,1)S(1)}, u32[]{:S(2)}) copy-start(pred[128,4,16]{2,1,0:T(4,128)(4,1)S(1)} %iota_compare_fusion.9) | copy-start | bytes 24580
  119.5 12.0 %copy-start.5 = (s32[128,512]{1,0:T(8,128)S(1)}, s32[128,512]{1,0:T(8,128)}, u32[]{:S(2)}) copy-start(s32[128,512]{1,0:T(8,128)} %param.20) | copy-start | bytes 786436
  119.5 12.2 %copy-start.11 = (bf16[4,128,128]{2,1,0:T(8,128)(2,1)S(1)}, bf16[4,128,128]{2,1,0:T(8,128)(2,1)}, u32[]{:S(2)}) copy-start(bf16[4,128,128]{2,1,0:T(8,128)(2,1)} %param.23) | copy-start | bytes 393220
  119.5 12.8 %copy-start.13 = (bf16[128,128]{1,0:T(8,128)(2,1)S(1)}, bf16[128,128]{1,0:T(8,128)(2,1)}, u32[]{:S(2)}) copy-start(bf16[128,128]{1,0:T(8,128)(2,1)} %param.22) | copy-start | bytes 98308
  119.5 12.8 %copy-start.9 = (bf16[4,128,128]{2,1,0:T(8,128)(2,1)S(1)}, bf16[4,128,128]{2,1,0:T(8,128)(2,1)}, u32[]{:S(2)}) copy-start(bf16[4,128,128]{2,1,0:T(8,128)(2,1)} %param.24) | copy-start | bytes 393220
  119.5 42.2 %all-to-all-start = ((bf16[4,128,16,128]{3,2,0,1:T(8,128)(2,1)}), bf16[4,128,16,128]{3,2,0,1:T(8,128)(2,1)}, u32[]{:S(2)}, u32[]{:S(2)}) async-start(bf16[4,128,16,128]{3,2,0,1:T(8,128)(2,1)} %convert_bitcast_fusion), calls=%async_computation | async-start | bytes 4194304 | tf_op jit(solution)/shard_map/all_to_all | solution.py:171
  170.6 2.5 copy-start.12
  173.8 1.7 copy-start.8
  181.5 8.9 %collective-permute-start = (bf16[1,2,128,128]{3,2,1,0:T(8,128)(2,1)S(1)}, bf16[1,2,128,128]{3,2,1,0:T(8,128)(2,1)S(1)}, u32[]{:S(2)}, u32[]{:S(2)}) collective-permute-start(bf16[1,2,128,128]{3,2,1,0:T(8,128)(2,1)S(1)} %get-tuple-element.106), channel_id=1, source_target_pairs={{0,4},{4,8},{8,12},{12,16},{16,20},{20,24},{24,28},{28,32},{32,36}... | collective-permute-start | bytes 196616 | tf_op jit(solution)/shard_map/ppermute | solution.py:20
  184.3 6.1 %collective-permute-start.1 = (bf16[1,2,128,128]{3,2,1,0:T(8,128)(2,1)S(1)}, bf16[1,2,128,128]{3,2,1,0:T(8,128)(2,1)S(1)}, u32[]{:S(2)}, u32[]{:S(2)}) collective-permute-start(bf16[1,2,128,128]{3,2,1,0:T(8,128)(2,1)S(1)} %get-tuple-element.107), channel_id=1, source_target_pairs={{4,0},{8,4},{12,8},{16,12},{20,16},{24,20},{28,24},{32,28},{36,32}... | collective-permute-start | bytes 196616 | tf_op jit(solution)/shard_map/ppermute | solution.py:23
  190.5 10.2 %collective-permute-start.2 = (bf16[4,1,128,128]{3,2,1,0:T(8,128)(2,1)S(1)}, bf16[4,1,128,128]{3,2,1,0:T(8,128)(2,1)S(1)}, u32[]{:S(2)}, u32[]{:S(2)}) collective-permute-start(bf16[4,1,128,128]{3,2,1,0:T(8,128)(2,1)S(1)} %get-tuple-element.101), channel_id=1, source_target_pairs={{0,1},{1,2},{2,3},{4,5},{5,6},{6,7},{8,9},{9,10},{10,11},{12,13},{... | collective-permute-start | bytes 393224 | tf_op jit(solution)/shard_map/ppermute | solution.py:20
  192.9 7.8 %collective-permute-start.3 = (bf16[4,1,128,128]{3,2,1,0:T(8,128)(2,1)S(1)}, bf16[4,1,128,128]{3,2,1,0:T(8,128)(2,1)S(1)}, u32[]{:S(2)}, u32[]{:S(2)}) collective-permute-start(bf16[4,1,128,128]{3,2,1,0:T(8,128)(2,1)S(1)} %get-tuple-element.100), channel_id=1, source_target_pairs={{1,0},{2,1},{3,2},{5,4},{6,5},{7,6},{9,8},{10,9},{11,10},{13,12},{... | collective-permute-start | bytes 393224 | tf_op jit(solution)/shard_map/ppermute | solution.py:23
  200.7 0.9 copy-start.7
  200.8 1.3 copy-start.14
  200.9 1.6 copy-start.10
  207.6 2.2 copy-start.3
  287.7 39.0 %copy-start.16 = (pred[128,4,16]{2,1,0:T(4,128)(4,1)S(1)}, pred[128,4,16]{2,1,0:T(4,128)(4,1)}, u32[]{:S(2)}) copy-start(pred[128,4,16]{2,1,0:T(4,128)(4,1)} %copy-done.15) | copy-start | bytes 24580
  287.7 39.0 %all-to-all-start.1 = ((bf16[128,4,1,16,128]{4,3,1,2,0:T(8,128)(2,1)}), bf16[128,4,1,16,128]{4,3,1,2,0:T(8,128)(2,1)S(1)}, u32[]{:S(2)}, u32[]{:S(2)}) async-start(bf16[128,4,1,16,128]{4,3,1,2,0:T(8,128)(2,1)} %constant_dynamic-update-slice_fusion.8), calls=%async_computation.1 | async-start | bytes 4194304 | tf_op jit(solution)/shard_map/all_to_all | solution.py:229
  296.2 36.1 %copy-start.6 = (s32[128,32]{1,0:T(8,128)}, s32[128,32]{1,0:T(8,128)S(1)}, u32[]{:S(2)}) copy-start(s32[128,32]{1,0:T(8,128)S(1)} %reshape.205) | copy-start | bytes 49156
  353.4 1.0 copy-start.4
  353.4 1.6 copy-start.1
